TPU v7x, 256 devices: a whole 4x4x8 slice. The times are simulated.
256 devices in a mesh: row: 32 (over x_lo, z, core), col: 8 (over x_hi, y).
Axes of the slice: x: 4 (x_hi: 2, x_lo: 2; x = x_hi * 2 + x_lo), y: 4, z: 8, core: 2. Of those that a mesh axis runs over, the one named last changes fastest.
Arguments:
- rhs: float32 [2031616], P(('row', 'col')), may hold values from -6 to 6
- blocks: float32 [32, 8, 64, 128, 128], P('row', 'col'), may hold values from -0.5 to 0.5
- blk_row: int32 [32, 8, 64], P('row', 'col'), may hold values from 0 to 495
- blk_col: int32 [32, 8, 64], P('row', 'col'), may hold values from 0 to 511
Outputs:
- solution: float32 [524288], P(('col', 'row'))
- rel_residual: float32 [], replicated
Inputs may be any that keep to these rules, and one draw needn't show every extreme that they name: `blk_row`: each device holds 64 blocks; blocks listed twice at the same place are added.
All inputs are finite; a program needn't handle non-finite values.
Results may differ from a plain program's by a relative error of at most 0.00013.
Values sent between devices are 32-bit elements; how exact they have to be, the bound alone decides.
A program may use at most 64 MiB of HBM per device.

v0:
```python
import jax
import jax.numpy as jnp
from jax import lax
from jax.sharding import PartitionSpec as P

BLK = 128
ROWB_DEV = 496
COLB_DEV = 512
NB_DEV = 64
ITERS = 3


def on_device(rhs, blocks, blk_row, blk_col):
    tiles = blocks.reshape(NB_DEV, BLK, BLK)
    rows_at = blk_row.reshape(NB_DEV)
    cols_at = blk_col.reshape(NB_DEV)

    def fwd_local(whole):
        picked = whole.reshape(COLB_DEV, BLK)[cols_at]
        prod = jnp.einsum("nij,nj->ni", tiles, picked, precision=lax.Precision.HIGHEST)
        total = jnp.zeros((ROWB_DEV, BLK), jnp.float32).at[rows_at].add(prod)
        return total.reshape(ROWB_DEV * BLK)

    def back_local(whole):
        picked = whole.reshape(ROWB_DEV, BLK)[rows_at]
        prod = jnp.einsum("nij,ni->nj", tiles, picked, precision=lax.Precision.HIGHEST)
        total = jnp.zeros((COLB_DEV, BLK), jnp.float32).at[cols_at].add(prod)
        return total.reshape(COLB_DEV * BLK)

    def forward(vec):
        whole = lax.all_gather(vec, "row", axis=0, tiled=True)
        return lax.psum_scatter(fwd_local(whole), "col", scatter_dimension=0, tiled=True)

    def backward(vec):
        whole = lax.all_gather(vec, "col", axis=0, tiled=True)
        return lax.psum_scatter(back_local(whole), "row", scatter_dimension=0, tiled=True)

    def u_length(vec):
        return jnp.sqrt(lax.psum(jnp.sum(vec * vec), ("row", "col")))

    def settle_u(raw):
        beta = u_length(raw)
        unit = raw / beta
        return (unit, beta, backward(unit))

    def settle_v(raw, needed):
        alpha = u_length(raw)
        unit = raw / alpha
        front = forward(unit) if needed else None
        return (unit, alpha, front)

    u, beta_first, back = settle_u(rhs)
    v, alpha, front = settle_v(back, True)
    w = v
    solution = jnp.zeros_like(v)
    phibar = beta_first
    rhobar = alpha
    for step in range(ITERS):
        u, beta, back = settle_u(front - alpha * u)
        v, alpha, front = settle_v(back - beta * v, step + 1 < ITERS)
        rho = jnp.sqrt(rhobar * rhobar + beta * beta)
        cosine = rhobar / rho
        sine = beta / rho
        theta = sine * alpha
        rhobar = -cosine * alpha
        phi = cosine * phibar
        phibar = sine * phibar
        solution = solution + phi / rho * w
        w = v - theta / rho * w
    return (solution, phibar / beta_first)


def solution(mesh):
    return jax.shard_map(
        on_device,
        mesh=mesh,
        in_specs=(
            P(("row", "col")),
            P("row", "col", None, None, None),
            P("row", "col", None),
            P("row", "col", None),
        ),
        out_specs=(P(("col", "row")), P()),
        check_vma=False,
    )
```

profile of v0, /device:TPU:1, one launch (start us, length us, event | category | flops | bytes accessed | tf_op | source)
XLA Modules:
  0.0 1724.2 jit_solution(6133877332784568407)
XLA Ops:
  7.2 0.0 all-reduce.13.cloned.1.call-start
  7.2 1.4 multiply_reduce_fusion.2
  8.6 81.4 %psum.49 = f32[]{:T(128)} all-reduce(f32[]{:T(128)} %multiply_reduce_fusion.2), channel_id=1, replica_groups=mesh['row'=32,'col'=8] {'row','col'}, use_global_device_ids=true, to_apply=%region_1.0 | all-reduce | flops 1 | bytes 8 | tf_op jit(solution)/shard_map/psum | solution.py:39
  90.7 0.8 broadcast_divide_fusion.2
  91.5 28.0 %all-gather = f32[8,1,7936]{2,1,0:T(1,128)S(1)} all-gather(f32[1,1,7936]{2,1,0:T(1,128)S(1)} %reshape.216), channel_id=1, replica_groups=mesh['row'=32,'col'=8] {'col'}, dimensions={0}, use_global_device_ids=true | all-gather | bytes 285696 | tf_op jit(solution)/shard_map/all_gather | solution.py:35
  119.5 0.7 fusion.27
  120.2 0.7 fusion.26
  120.8 0.6 gather_fusion
  121.4 5.3 fusion.10
  126.7 1.5 scatter_custom_fusion
  128.2 0.0 all-reduce.13.cloned.1.call-update
  128.2 0.0 all-reduce.15.cloned.1.call-start
  128.3 0.6 dynamic-slice
  129.5 220.2 %all-reduce.13.cloned.1.call-done = f32[65536]{0:T(1024)} async-done(((f32[65536]{0:T(1024)}), f32[65536]{0:T(1024)}) %all-reduce.13.cloned.1.call-update) | async-done | bytes 262160
  349.7 1.3 multiply_reduce_fusion.5
  351.0 77.7 %psum.50 = f32[]{:T(128)} all-reduce(f32[]{:T(128)} %multiply_reduce_fusion.5), channel_id=1, replica_groups=mesh['row'=32,'col'=8] {'row','col'}, use_global_device_ids=true, to_apply=%region_5.0 | all-reduce | flops 1 | bytes 8 | tf_op jit(solution)/shard_map/psum | solution.py:39
  429.3 0.7 dynamic-slice_divide_fusion
  430.1 31.9 %all_gather.19 = f32[65536]{0:T(1024)S(1)} all-gather(f32[2048]{0:T(1024)S(1)} %dynamic-slice_divide_fusion), channel_id=1, replica_groups=mesh['row'=32,'col'=8] {'row'}, dimensions={0}, use_global_device_ids=true | all-gather | bytes 270336 | tf_op jit(solution)/shard_map/all_gather | solution.py:31
  461.9 0.6 gather_fusion.1
  462.5 8.3 fusion.8
  470.8 1.5 scatter_custom_fusion.1
  472.3 0.0 all-reduce.15.cloned.1.call-update
  472.3 0.0 all-reduce.17.cloned.1.call-start
  472.4 0.6 dynamic-slice.2
  473.6 76.3 %all-reduce.15.cloned.1.call-done = f32[63488]{0:T(1024)} async-done(((f32[63488]{0:T(1024)}), f32[63488]{0:T(1024)}) %all-reduce.15.cloned.1.call-update) | async-done | bytes 253968
  550.0 1.5 multiply_reduce_fusion.1
  551.4 79.4 %psum.51 = f32[]{:T(128)} all-reduce(f32[]{:T(128)} %multiply_reduce_fusion.1), channel_id=1, replica_groups=mesh['row'=32,'col'=8] {'row','col'}, use_global_device_ids=true, to_apply=%region_9.0 | all-reduce | flops 1 | bytes 8 | tf_op jit(solution)/shard_map/psum | solution.py:39
  631.5 0.9 broadcast_divide_fusion.1
  632.4 28.3 %all-gather.1 = f32[8,1,7936]{2,1,0:T(1,128)S(1)} all-gather(f32[1,1,7936]{2,1,0:T(1,128)S(1)} %reshape.218), channel_id=1, replica_groups=mesh['row'=32,'col'=8] {'col'}, dimensions={0}, use_global_device_ids=true | all-gather | bytes 285696 | tf_op jit(solution)/shard_map/all_gather | solution.py:35
  660.6 0.6 gather_fusion.2
  661.2 5.3 fusion.6
  666.5 1.5 scatter_custom_fusion.2
  668.0 0.0 all-reduce.17.cloned.1.call-update
  668.0 0.0 all-reduce.19.cloned.1.call-start
  668.1 223.1 %all-reduce.17.cloned.1.call-done = f32[65536]{0:T(1024)} async-done(((f32[65536]{0:T(1024)}), f32[65536]{0:T(1024)}) %all-reduce.17.cloned.1.call-update) | async-done | bytes 262160
  891.1 1.3 multiply_reduce_fusion.4
  892.4 77.7 %psum.52 = f32[]{:T(128)} all-reduce(f32[]{:T(128)} %multiply_reduce_fusion.4), channel_id=1, replica_groups=mesh['row'=32,'col'=8] {'row','col'}, use_global_device_ids=true, to_apply=%region_13.0 | all-reduce | flops 1 | bytes 8 | tf_op jit(solution)/shard_map/psum | solution.py:39
  970.8 0.7 broadcast_divide_fusion.4
  971.5 32.0 %all_gather.21 = f32[65536]{0:T(1024)S(1)} all-gather(f32[2048]{0:T(1024)S(1)} %broadcast_divide_fusion.4), channel_id=1, replica_groups=mesh['row'=32,'col'=8] {'row'}, dimensions={0}, use_global_device_ids=true | all-gather | bytes 270336 | tf_op jit(solution)/shard_map/all_gather | solution.py:31
  1003.6 0.6 gather_fusion.3
  1004.2 8.3 fusion.4
  1012.5 1.5 scatter_custom_fusion.3
  1014.0 0.0 all-reduce.21.cloned.1.call-start
  1014.0 77.6 %all-reduce.19.cloned.1.call-done = f32[63488]{0:T(1024)} async-done(((f32[63488]{0:T(1024)}), f32[63488]{0:T(1024)}) %all-reduce.19.cloned.1.call-update) | async-done | bytes 253968
  1091.6 1.5 multiply_reduce_fusion
  1093.1 79.4 %psum.53 = f32[]{:T(128)} all-reduce(f32[]{:T(128)} %multiply_reduce_fusion), channel_id=1, replica_groups=mesh['row'=32,'col'=8] {'row','col'}, use_global_device_ids=true, to_apply=%region_17.0 | all-reduce | flops 1 | bytes 8 | tf_op jit(solution)/shard_map/psum | solution.py:39
  1173.1 0.9 broadcast_divide_fusion
  1174.0 28.3 %all-gather.2 = f32[8,1,7936]{2,1,0:T(1,128)S(1)} all-gather(f32[1,1,7936]{2,1,0:T(1,128)S(1)} %reshape.220), channel_id=1, replica_groups=mesh['row'=32,'col'=8] {'col'}, dimensions={0}, use_global_device_ids=true | all-gather | bytes 285696 | tf_op jit(solution)/shard_map/all_gather | solution.py:35
  1202.3 0.6 gather_fusion.4
  1202.9 5.3 fusion.2
  1208.1 1.5 scatter_custom_fusion.4
  1209.7 0.0 all-reduce.23.cloned.1.call-start
  1209.7 223.1 %all-reduce.21.cloned.1.call-done = f32[65536]{0:T(1024)} async-done(((f32[65536]{0:T(1024)}), f32[65536]{0:T(1024)}) %all-reduce.21.cloned.1.call-update) | async-done | bytes 262160
  1432.8 1.3 multiply_reduce_fusion.3
  1434.1 77.7 %psum.54 = f32[]{:T(128)} all-reduce(f32[]{:T(128)} %multiply_reduce_fusion.3), channel_id=1, replica_groups=mesh['row'=32,'col'=8] {'row','col'}, use_global_device_ids=true, to_apply=%region_21.0 | all-reduce | flops 1 | bytes 8 | tf_op jit(solution)/shard_map/psum | solution.py:39
  1512.4 0.7 broadcast_divide_fusion.3
  1513.1 31.9 %all_gather.23 = f32[65536]{0:T(1024)S(1)} all-gather(f32[2048]{0:T(1024)S(1)} %broadcast_divide_fusion.3), channel_id=1, replica_groups=mesh['row'=32,'col'=8] {'row'}, dimensions={0}, use_global_device_ids=true | all-gather | bytes 270336 | tf_op jit(solution)/shard_map/all_gather | solution.py:31
  1545.0 0.6 gather_fusion.5
  1545.6 8.3 fusion
  1553.9 1.5 scatter_custom_fusion.5
  1555.8 77.2 %all-reduce.23.cloned.1.call-done = f32[63488]{0:T(1024)} async-done(((f32[63488]{0:T(1024)}), f32[63488]{0:T(1024)}) %all-reduce.23.cloned.1.call-update) | async-done | bytes 253968
  1633.0 1.5 fusion.25
  1634.5 79.4 %psum.55 = f32[]{:T(128)} all-reduce(f32[]{:T(128)} %fusion.25), channel_id=1, replica_groups=mesh['row'=32,'col'=8] {'row','col'}, use_global_device_ids=true, to_apply=%region_25.0 | all-reduce | flops 1 | bytes 8 | tf_op jit(solution)/shard_map/psum | solution.py:39
  1714.9 1.3 multiply_add_fusion
  (14 shorter events, 0.1 us)
Async XLA Ops:
  7.2 121.1 %copy-start.2 = (u32[256]{0:T(256)S(1)}, u32[256]{0:T(256)}, u32[]{:S(2)}) copy-start(u32[256]{0:T(256)} %constant.15) | copy-start | bytes 3076
  7.2 342.5 %all-reduce.13.cloned.1.call-start = ((), (), s32[]{:S(2)}) async-start(), calls=%async_computation | async-start | bytes 524288
  121.4 351.0 %copy-start.1 = (u32[256]{0:T(256)S(1)}, u32[256]{0:T(256)}, u32[]{:S(2)}) copy-start(u32[256]{0:T(256)} %constant.19) | copy-start | bytes 3076
  121.4 428.5 %copy-start = (f32[7936]{0:T(1024)S(1)}, f32[7936]{0:T(1024)}, u32[]{:S(2)}) copy-start(f32[7936]{0:T(1024)} %param.4) | copy-start | bytes 95236
  128.2 421.7 %all-reduce.15.cloned.1.call-start = ((), (), s32[]{:S(2)}) async-start(), calls=%async_computation.1 | async-start | bytes 507904
  472.3 418.8 %all-reduce.17.cloned.1.call-start = ((), (), s32[]{:S(2)}) async-start(), calls=%async_computation.2 | async-start | bytes 524288
  668.0 423.6 %all-reduce.19.cloned.1.call-start = ((), (), s32[]{:S(2)}) async-start(), calls=%async_computation.3 | async-start | bytes 507904
  1014.0 418.8 %all-reduce.21.cloned.1.call-start = ((), (), s32[]{:S(2)}) async-start(), calls=%async_computation.4 | async-start | bytes 524288
  1209.7 423.4 %all-reduce.23.cloned.1.call-start = ((), (), s32[]{:S(2)}) async-start(), calls=%async_computation.5 | async-start | bytes 507904
Sparse Core Ops, SparseCore 0:
  128.3 221.2 all-reduce.12
  472.4 77.4 all-reduce.14
  668.1 222.9 all-reduce.16
  1014.1 77.4 all-reduce.18
  1209.8 222.9 all-reduce.20
  1555.5 77.4 all-reduce.22
where the time goes:
time: 1730 us; the launch traced here: 1720 us
  waiting for transfers between devices  898 us (52%)
  blocking collectives  733 us (42%)
  matrix products  40.7 us (2%)
  other arithmetic  25.8 us (1%)
  between operations  22.1 us (1%)
    unnamed x12, waiting for transfers between devices  898 us
    psum x7, blocking collectives, u_length(): return jnp.sqrt(lax.psum(jnp.sum(vec * vec), ('row', 'col')))  553 us
    all_gather x3, blocking collectives, forward(): whole = lax.all_gather(vec, 'row', axis=0, tiled=True)  95.7 us
    all_gather x3, blocking collectives, backward(): whole = lax.all_gather(vec, 'col', axis=0, tiled=True)  84.5 us
  transfers between devices with their start and end apart: 6, of which 6 were waited for; matrix products, arithmetic and copies ran while one was open for 0% of the time, Pallas kernels for 0%

commit v1 on v0

v1 whole, which is shorter than its diff:
```python
import functools

import jax
import jax.numpy as jnp
from jax import lax
from jax.experimental import pallas as pl
from jax.experimental.pallas import tpu as pltpu
from jax.sharding import PartitionSpec as P

BLK = 128
NB = 64
ITERS = 3
N_COL = 8
N_CHIP = 16
PER_COL = 62
MESH = pl.DeviceIdType.MESH
F32 = jnp.float32
BF16 = jnp.bfloat16
MSG = NB + 1
PIECE = 17
UNROLL = 8


def split3(x):
    hi = x.astype(BF16)
    rest = x - hi.astype(F32)
    mid = rest.astype(BF16)
    low = (rest - mid.astype(F32)).astype(BF16)
    return hi, mid, low


def total_of(x):
    return jnp.broadcast_to(jnp.sum(jnp.sum(x, axis=0, keepdims=True), axis=1, keepdims=True), (1, BLK))


def kernel(rows_at, cols_at, rhs, index, blocks_hbm, sol_out, rel_out,
           blocks, u, v, v_old, put_rows, put_cols, parts,
           col_src, col_dst, core_src, core_dst, rs_src, rs_dst, vb, ids, fin_src, fin_dst, w, sol,
           blk_sem, col_send, col_recv, core_send, core_recv, rs_send, rs_recv, ag_send, ag_recv,
           half_send, half_recv, ids_send, ids_recv, fin_send, fin_recv, finc_send, finc_recv, fin_core):
    r = lax.axis_index("row")
    c = lax.axis_index("col")
    q = r // 2
    h = lax.rem(r, 2)
    other = q * 2 + (1 - h)
    partner = {"row": other, "col": c}

    load = pltpu.make_async_copy(blocks_hbm, blocks, blk_sem)
    load.start()

    def col_peer(d):
        return {"row": r, "col": lax.rem(c + d, N_COL)}

    def chip_of(d):
        return lax.rem(q + d, N_CHIP)

    barrier = pltpu.get_barrier_semaphore()
    for d in range(1, N_COL):
        pl.semaphore_signal(barrier, inc=1, device_id=col_peer(d), device_id_type=MESH)
    for d in range(1, N_CHIP):
        pl.semaphore_signal(barrier, inc=1, device_id={"row": chip_of(d) * 2 + h, "col": c}, device_id_type=MESH)
    pl.semaphore_signal(barrier, inc=1, device_id=partner, device_id_type=MESH)

    col_src[0, 0:PER_COL, :] = rhs[...]
    col_src[0, PER_COL:NB, :] = jnp.zeros((NB - PER_COL, BLK), F32)
    col_src[0, NB:MSG, :] = index[...]
    pl.semaphore_wait(barrier, N_COL - 1 + N_CHIP - 1 + 1)

    def col_start(k):
        for d in range(1, N_COL):
            pltpu.make_async_remote_copy(
                src_ref=col_src.at[k], dst_ref=col_dst.at[k, c], send_sem=col_send.at[k], recv_sem=col_recv.at[k],
                device_id=col_peer(d), device_id_type=MESH).start()

    def col_wait(k):
        pltpu.make_async_copy(col_dst.at[k, pl.ds(0, N_COL - 1)], col_dst.at[k, pl.ds(0, N_COL - 1)], col_recv.at[k]).wait()

    ids_copy = pltpu.make_async_remote_copy(
        src_ref=index, dst_ref=ids, send_sem=ids_send, recv_sem=ids_recv, device_id=partner, device_id_type=MESH)
    col_start(0)
    ids_copy.start()

    sub = lax.broadcasted_iota(jnp.int32, (BLK, BLK), 0)
    lane = lax.broadcasted_iota(jnp.int32, (BLK, BLK), 1)
    eye = sub == lane
    lane1 = lax.broadcasted_iota(jnp.int32, (1, BLK), 1)
    low_half = lane1 < NB

    v_old[...] = jnp.zeros((512, BLK), F32)
    w[...] = jnp.zeros((16, BLK), F32)
    sol[...] = jnp.zeros((16, BLK), F32)
    col_dst[0, c] = col_src[0]

    ids_copy.wait()
    mine = index[...]
    theirs = ids[...]
    first = jnp.where(h == 0, mine, theirs)
    second = jnp.where(h == 0, theirs, mine)
    pair_cols = jnp.where(low_half, pltpu.roll(first, NB, 1), second)
    i256 = lax.broadcasted_iota(jnp.int32, (256, BLK), 0)
    owner_block = ((i256 // 16) * 32 + h * 16 + lax.rem(i256, 16)).astype(F32)
    put_cols[...] = jnp.where(owner_block == pair_cols, 1.0, 0.0).astype(BF16)

    col_wait(0)
    i512 = lax.broadcasted_iota(jnp.int32, (512, BLK), 0).astype(F32)
    for j in range(N_COL // 2):
        a = col_dst[0, 2 * j, NB:MSG, :]
        b = col_dst[0, 2 * j + 1, NB:MSG, :]
        pair = jnp.where(low_half, a, pltpu.roll(b, NB, 1))
        put_rows[:, j * BLK:(j + 1) * BLK] = jnp.where(i512 == pair, 1.0, 0.0).astype(BF16)
    for j in range(N_COL):
        u[j * NB:(j + 1) * NB, :] = col_dst[0, j, 0:NB, :]
    load.wait()

    def step(k, carry):
        rhobar, phibar, beta_first = carry
        su = total_of(u[...] * u[...])

        def back(g, _):
            for t in range(UNROLL):
                n = g * UNROLL + t
                row = u[pl.ds(rows_at[n], 1), :]
                column = jnp.sum(jnp.where(eye, row, 0.0), axis=1, keepdims=True)
                core_src[k, pl.ds(n, 1), :] = jnp.sum(blocks[n] * column, axis=0, keepdims=True)
            return 0
        lax.fori_loop(0, NB // UNROLL, back, 0)
        core_src[k, NB:MSG, :] = su
        swap = pltpu.make_async_remote_copy(
            src_ref=core_src.at[k], dst_ref=core_dst.at[k], send_sem=core_send.at[k], recv_sem=core_recv.at[k],
            device_id=partner, device_id_type=MESH)
        swap.start()
        for p, x in enumerate(split3(core_src[k, 0:NB, :])):
            parts[pl.ds(pl.multiple_of(h * NB, NB), NB), p * BLK:(p + 1) * BLK] = x
        swap.wait_recv()
        for p, x in enumerate(split3(core_dst[k, 0:NB, :])):
            parts[pl.ds(pl.multiple_of((1 - h) * NB, NB), NB), p * BLK:(p + 1) * BLK] = x
        dense = jnp.dot(put_cols[...], parts[0:2 * NB, :], preferred_element_type=F32)
        dense = dense[:, 0:BLK] + dense[:, BLK:2 * BLK] + dense[:, 2 * BLK:3 * BLK]
        both = su + core_dst[k, NB:MSG, :]
        for j in range(N_CHIP):
            rs_src[k, j, 0:16, :] = dense[j * 16:(j + 1) * 16, :]
            rs_src[k, j, 16:PIECE, :] = both
        for d in range(1, N_CHIP):
            there = chip_of(d)
            pltpu.make_async_remote_copy(
                src_ref=rs_src.at[k, there], dst_ref=rs_dst.at[k, q], send_sem=rs_send.at[k], recv_sem=rs_recv.at[k],
                device_id={"row": there * 2 + h, "col": c}, device_id_type=MESH).start()
        rs_dst[k, q] = rs_src[k, q]
        pltpu.make_async_copy(rs_dst.at[k, pl.ds(0, N_CHIP - 1)], rs_dst.at[k, pl.ds(0, N_CHIP - 1)], rs_recv.at[k]).wait()
        piece = rs_dst[k, 0]
        for j in range(1, N_CHIP):
            piece = piece + rs_dst[k, j]
        vb[k, q, h] = piece[0:16, :]
        for d in range(1, N_CHIP):
            pltpu.make_async_remote_copy(
                src_ref=vb.at[k, q, h], dst_ref=vb.at[k, q, h], send_sem=ag_send.at[k], recv_sem=ag_recv.at[k],
                device_id={"row": chip_of(d) * 2 + h, "col": c}, device_id_type=MESH).start()
        beta = jnp.sqrt(piece[16:17, :])
        u[...] = u[...] / beta
        beta_first = jnp.where(k == 0, beta, beta_first)
        pltpu.make_async_copy(vb.at[k, pl.ds(0, N_CHIP - 1), h], vb.at[k, pl.ds(0, N_CHIP - 1), h], ag_recv.at[k]).wait()
        give = pltpu.make_async_remote_copy(
            src_ref=vb.at[k, :, h], dst_ref=vb.at[k, :, h], send_sem=half_send.at[k], recv_sem=half_recv.at[k],
            device_id=partner, device_id_type=MESH)
        give.start()
        give.wait_recv()
        v[...] = vb[k].reshape(512, BLK) / beta - beta * v_old[...]
        sv = total_of(v[...] * v[...])

        def front(g, _):
            for t in range(UNROLL):
                n = g * UNROLL + t
                row = v[pl.ds(cols_at[n], 1), :]
                column = jnp.sum(blocks[n] * row, axis=1, keepdims=True)
                col_src[k + 1, pl.ds(n, 1), :] = jnp.sum(jnp.where(eye, column, 0.0), axis=0, keepdims=True)
            return 0
        lax.fori_loop(0, NB // UNROLL, front, 0)
        col_src[k + 1, NB:MSG, :] = sv
        col_start(k + 1)
        col_dst[k + 1, c] = col_src[k + 1]
        col_wait(k + 1)
        square = col_dst[k + 1, 0, NB:MSG, :]
        for j in range(1, N_COL):
            square = square + col_dst[k + 1, j, NB:MSG, :]
        alpha = jnp.sqrt(square)
        for j in range(N_COL):
            for p, x in enumerate(split3(col_dst[k + 1, j, 0:NB, :])):
                parts[j * NB:(j + 1) * NB, p * BLK:(p + 1) * BLK] = x
        front_sum = jnp.dot(put_rows[...], parts[...], preferred_element_type=F32)
        front_sum = front_sum[:, 0:BLK] + front_sum[:, BLK:2 * BLK] + front_sum[:, 2 * BLK:3 * BLK]
        u[...] = front_sum / alpha - alpha * u[...]
        v_old[...] = v[...] / alpha

        unit = v_old[pl.ds(pl.multiple_of(r * 16, 16), 16), :]
        rho = jnp.sqrt(rhobar * rhobar + beta * beta)
        cosine = rhobar / rho
        sine = beta / rho
        theta = sine * alpha
        phi = cosine * phibar
        w_now = w[...]
        sol[...] = sol[...] + phi / rho * w_now
        w[...] = unit - theta / rho * w_now
        rhobar = jnp.where(k == 0, alpha, -cosine * alpha)
        phibar = jnp.where(k == 0, beta, sine * phibar)
        return rhobar, phibar, beta_first

    one = jnp.ones((1, BLK), F32)
    rhobar, phibar, beta_first = lax.fori_loop(0, ITERS, step, (one, jnp.zeros((1, BLK), F32), one))

    su = total_of(u[...] * u[...])
    fin_src[0] = jnp.broadcast_to(su, (8, BLK))
    swap = pltpu.make_async_remote_copy(
        src_ref=fin_src.at[0], dst_ref=fin_core, send_sem=finc_send, recv_sem=finc_recv,
        device_id=partner, device_id_type=MESH)
    swap.start()
    swap.wait_recv()
    both = fin_src[0] + fin_core[...]
    fin_src[1] = both
    for d in range(1, N_CHIP):
        pltpu.make_async_remote_copy(
            src_ref=fin_src.at[1], dst_ref=fin_dst.at[q], send_sem=fin_send, recv_sem=fin_recv,
            device_id={"row": chip_of(d) * 2 + h, "col": c}, device_id_type=MESH).start()
    fin_dst[q] = both
    pltpu.make_async_copy(fin_dst.at[pl.ds(0, N_CHIP - 1)], fin_dst.at[pl.ds(0, N_CHIP - 1)], fin_recv).wait()
    square = fin_dst[0]
    for j in range(1, N_CHIP):
        square = square + fin_dst[j]
    beta = jnp.sqrt(square[0:1, :])
    rho = jnp.sqrt(rhobar * rhobar + beta * beta)
    phi = rhobar / rho * phibar
    sol_out[...] = sol[...] + phi / rho * w[...]
    rel_out[...] = jnp.broadcast_to(beta / rho * phibar / beta_first, (8, BLK))

    swap.wait_send()
    ids_wait = pltpu.make_async_copy(fin_dst.at[pl.ds(0, N_CHIP - 1)], fin_dst.at[pl.ds(0, N_CHIP - 1)], fin_send)
    ids_wait.wait()

    def drain_col(k, _):
        pltpu.make_async_copy(col_dst.at[k, pl.ds(0, N_COL - 1)], col_dst.at[k, pl.ds(0, N_COL - 1)], col_send.at[k]).wait()
        return 0
    lax.fori_loop(0, ITERS + 1, drain_col, 0)

    def drain_row(k, _):
        pltpu.make_async_copy(core_dst.at[k], core_dst.at[k], core_send.at[k]).wait()
        pltpu.make_async_copy(rs_dst.at[k, pl.ds(0, N_CHIP - 1)], rs_dst.at[k, pl.ds(0, N_CHIP - 1)], rs_send.at[k]).wait()
        pltpu.make_async_copy(vb.at[k, pl.ds(0, N_CHIP - 1), h], vb.at[k, pl.ds(0, N_CHIP - 1), h], ag_send.at[k]).wait()
        pltpu.make_async_copy(vb.at[k, :, h], vb.at[k, :, h], half_send.at[k]).wait()
        return 0
    lax.fori_loop(0, ITERS, drain_row, 0)


def on_device(rhs, blocks, blk_row, blk_col):
    rows = blk_row.reshape(NB)
    rows = rows // PER_COL * NB + rows % PER_COL
    cols = blk_col.reshape(NB)
    index = jnp.concatenate([rows, cols]).astype(F32).reshape(1, BLK)
    vmem = pl.BlockSpec(memory_space=pltpu.VMEM)
    smem = pl.BlockSpec(memory_space=pltpu.SMEM)
    dma = pltpu.SemaphoreType.DMA
    sol, rel = pl.pallas_call(
        kernel,
        out_shape=(jax.ShapeDtypeStruct((16, BLK), F32), jax.ShapeDtypeStruct((8, BLK), F32)),
        in_specs=[smem, smem, vmem, vmem, pl.BlockSpec(memory_space=pl.ANY)],
        out_specs=(vmem, vmem),
        scratch_shapes=[
            pltpu.VMEM((NB, BLK, BLK), F32),
            pltpu.VMEM((512, BLK), F32),
            pltpu.VMEM((512, BLK), F32),
            pltpu.VMEM((512, BLK), F32),
            pltpu.VMEM((512, 512), BF16),
            pltpu.VMEM((256, BLK), BF16),
            pltpu.VMEM((512, 3 * BLK), BF16),
            pltpu.VMEM((ITERS + 1, MSG, BLK), F32),
            pltpu.VMEM((ITERS + 1, N_COL, MSG, BLK), F32),
            pltpu.VMEM((ITERS, MSG, BLK), F32),
            pltpu.VMEM((ITERS, MSG, BLK), F32),
            pltpu.VMEM((ITERS, N_CHIP, PIECE, BLK), F32),
            pltpu.VMEM((ITERS, N_CHIP, PIECE, BLK), F32),
            pltpu.VMEM((ITERS, N_CHIP, 2, 16, BLK), F32),
            pltpu.VMEM((1, BLK), F32),
            pltpu.VMEM((2, 8, BLK), F32),
            pltpu.VMEM((N_CHIP, 8, BLK), F32),
            pltpu.VMEM((16, BLK), F32),
            pltpu.VMEM((16, BLK), F32),
            dma, dma((ITERS + 1,)), dma((ITERS + 1,)), dma((ITERS,)), dma((ITERS,)), dma((ITERS,)), dma((ITERS,)),
            dma((ITERS,)), dma((ITERS,)), dma((ITERS,)), dma((ITERS,)), dma, dma, dma, dma, dma, dma,
            pltpu.VMEM((8, BLK), F32),
        ],
        compiler_params=pltpu.CompilerParams(
            collective_id=0, has_side_effects=True, vmem_limit_bytes=48 * 1024 * 1024),
    )(rows, cols, rhs.reshape(PER_COL, BLK), index, blocks.reshape(NB, BLK, BLK))
    return sol.reshape(16 * BLK), rel[0, 0]


def solution(mesh):
    return jax.shard_map(
        on_device,
        mesh=mesh,
        in_specs=(
            P(("row", "col")),
            P("row", "col", None, None, None),
            P("row", "col", None),
            P("row", "col", None),
        ),
        out_specs=(P(("col", "row")), P()),
        check_vma=False,
    )
```

time: 1730 us -> 109 us (0.06)
  waiting for transfers between devices: 898 us -> 0 us
  blocking collectives: 733 us -> 0 us
  Pallas kernels: 0 us -> 101 us
  matrix products: 40.7 us -> 0 us
  other arithmetic: 25.8 us -> 2.08 us
  between operations: 22.1 us -> 0.65 us
    unnamed x12 -> x0, waiting for transfers between devices: 898 us -> none
    psum x7 -> x0, blocking collectives: 553 us -> none  [u_length(): return jnp.sqrt(lax.psum(jnp.sum(vec * vec), ('row', 'col')))]
    all_gather x6 -> x0, blocking collectives: 180 us -> none  [the longest x3 95.7 us: forward(): whole = lax.all_gather(vec, 'row', axis=0, tiled=True)]
    pallas_call x0 -> x1, Pallas kernels: none -> 101 us  [on_device(): pl.pallas_call(kernel, out_shape=(jax.ShapeDtypeStruct((16, BLK), F32), j...]
    dot_general x6 -> x0, matrix products: 40.7 us -> none  [the longest x3 24.9 us: fwd_local(): jnp.einsum('nij,nj->ni', tiles, picked, precision=lax.Precision.HIGHEST)]
  transfers between devices with their start and end apart: 6 -> 0, of which waited for: 6 -> 0; matrix products, arithmetic and copies ran while one was open for 0% -> 0% of each run, Pallas kernels for 0% -> 0%
where the time goes in v1:
time: 109 us
  Pallas kernels  101 us (93%)
  local copies, waits for them, and re-layouts  4.71 us (4%)
  other arithmetic  2.08 us (2%)
    pallas_call x1, Pallas kernels, on_device(): pl.pallas_call(kernel, out_shape=(jax.ShapeDtypeStruct((16, BLK), F32), j...  101 us
    unnamed x7, local copies, waits for them, and re-layouts  4.19 us

profile of v1, /device:TPU:1, one launch (start us, length us, event | category | flops | bytes accessed | tf_op | source)
XLA Modules:
  0.0 108.7 jit_solution(827780312496070635)
XLA Ops:
  0.6 0.7 fusion.2
  1.3 0.7 add_convert_fusion.index
  2.0 0.7 fusion.1.rows_at
  2.7 0.0 copy-start
  2.7 2.2 %copy-done = f32[1,1,64,128,128]{4,3,2,1,0:T(8,128)S(1)} copy-done((f32[1,1,64,128,128]{4,3,2,1,0:T(8,128)S(1)}, f32[1,1,64,128,128]{4,3,2,1,0:T(8,128)}, u32[]{:S(2)}) %copy-start) | copy-done | bytes 4194328
  4.9 0.0 copy-start.1
  4.9 0.8 copy-done.1
  5.7 0.0 copy-start.2
  5.7 0.7 copy-done.2
  6.3 101.3 %shard_map.59 = (f32[16,128]{1,0:T(8,128)S(1)}, f32[8,128]{1,0:T(8,128)S(1)}) custom-call(s32[64]{0:T(128)S(1)} %fusion.1.rows_at, s32[64]{0:T(128)S(1)} %bitcast.33, f32[62,128]{1,0:T(8,128)S(1)} %bitcast.30, f32[1,128]{1,0:T(1,128)S(1)} %add_convert_fusion.index, f32[64,128,128]{2,1,0:T(8,128)S(1)} %bitcast.29), custom_call_target="tpu_custom_call" | custom-call | tf_op jit(solution)/shard_map/pallas_call | solution.py:260
  107.6 0.5 slice.3
  108.1 0.6 copy.7
Async XLA Ops:
  2.7 2.2 %copy-start = (f32[1,1,64,128,128]{4,3,2,1,0:T(8,128)S(1)}, f32[1,1,64,128,128]{4,3,2,1,0:T(8,128)}, u32[]{:S(2)}) copy-start(f32[1,1,64,128,128]{4,3,2,1,0:T(8,128)} %param.5) | copy-start | bytes 12582916
  4.9 0.8 copy-start.1
  5.7 0.7 copy-start.2

commit v2 on v0

v2 whole, which is shorter than its diff:
```python
import jax
import jax.numpy as jnp
from jax import lax
from jax.experimental import pallas as pl
from jax.experimental.pallas import tpu as pltpu
from jax.sharding import PartitionSpec as P

BLK = 128
NB = 64
ITERS = 3
N_ROW = 32
N_COL = 8
N_CHIP = 16
ROWB = 496
COLB = 512
PER_COL = 62
MESH = pl.DeviceIdType.MESH
F32 = jnp.float32
BF16 = jnp.bfloat16
MSG = NB + 1
PIECE = 17
UNROLL = 8


def ring(d, n):
    return min(d % n, n - d % n)


CHIPS = sorted(((x, z) for x in range(2) for z in range(8) if (x, z) != (0, 0)), key=lambda t: -(t[0] + ring(t[1], 8)))
CORES = sorted(
    ((x, z, s) for x in range(2) for z in range(8) for s in range(2) if (x, z, s) != (0, 0, 0)),
    key=lambda t: -(t[0] + ring(t[1], 8) + 0.1 * t[2]))
COLS = sorted(((x, y) for x in range(2) for y in range(4) if (x, y) != (0, 0)), key=lambda t: -(4 * t[0] + ring(t[1], 4)))


def split3(x):
    hi = x.astype(BF16)
    rest = x - hi.astype(F32)
    mid = rest.astype(BF16)
    low = (rest - mid.astype(F32)).astype(BF16)
    return hi, mid, low


def join3(x):
    return x[:, 0:BLK] + x[:, BLK:2 * BLK] + x[:, 2 * BLK:3 * BLK]


def total_of(x):
    return jnp.broadcast_to(jnp.sum(jnp.sum(x, axis=0, keepdims=True), axis=1, keepdims=True), (1, BLK))


def kernel(rows_hbm, cols_hbm, rhs_hbm, blocks_hbm, sol_out, rel_out,
           raw, tiles, u, v, picks, spread, sums, put_rows, put_cols, parts, parts2,
           col_src, col_dst, core_src, core_dst, rs_src, rs_dst, vb, ids_src, ids_dst, fin_src, fin_dst, w, sol, start,
           rows_v, cols_v, rows_at, cols_at,
           load_sem, col_send, near_recv, far_recv, core_send, core_recv, rs_send, rs_recv, ag_send, ag_recv,
           half_send, half_recv, ids_send, ids_recv, fin_send, fin_recv):
    r = lax.axis_index("row")
    c = lax.axis_index("col")
    q = r // 2
    h = lax.rem(r, 2)
    x_low = q // 8
    z = lax.rem(q, 8)
    side = c // 4
    y = lax.rem(c, 4)
    partner = {"row": q * 2 + (1 - h), "col": c}

    def chip_at(dx, dz):
        return lax.rem(x_low + dx, 2) * 8 + lax.rem(z + dz, 8)

    def row_peer(dx, dz, dh):
        return {"row": chip_at(dx, dz) * 2 + lax.rem(h + dh, 2), "col": c}

    def col_peer(dx, dy):
        return {"row": r, "col": lax.rem(side + dx, 2) * 4 + lax.rem(y + dy, 4)}

    barrier = pltpu.get_barrier_semaphore()
    for d in CORES:
        pl.semaphore_signal(barrier, inc=1, device_id=row_peer(*d), device_id_type=MESH)
    for d in COLS:
        pl.semaphore_signal(barrier, inc=1, device_id=col_peer(*d), device_id_type=MESH)

    loads = [
        pltpu.make_async_copy(rows_hbm, rows_v, load_sem.at[0]),
        pltpu.make_async_copy(cols_hbm, cols_v, load_sem.at[1]),
        pltpu.make_async_copy(rhs_hbm, col_src.at[0, pl.ds(0, PER_COL)], load_sem.at[2]),
        pltpu.make_async_copy(rows_hbm, rows_at, load_sem.at[3]),
        pltpu.make_async_copy(cols_hbm, cols_at, load_sem.at[4]),
        pltpu.make_async_copy(blocks_hbm, raw, load_sem.at[5]),
    ]
    for copy in loads:
        copy.start()
    col_src[0, PER_COL:MSG, :] = jnp.zeros((MSG - PER_COL, BLK), F32)
    ids_src[...] = jnp.zeros((1, BLK), F32)
    loads[0].wait()
    loads[1].wait()
    col_src[0, NB:MSG, 0:NB] = rows_v[...].astype(F32)
    ids_src[:, 0:NB] = cols_v[...].astype(F32)
    loads[2].wait()
    pl.semaphore_wait(barrier, len(CORES) + len(COLS))

    def col_start(k):
        for d in COLS:
            pltpu.make_async_remote_copy(
                src_ref=col_src.at[k], dst_ref=col_dst.at[k, c], send_sem=col_send.at[k],
                recv_sem=(far_recv if d[0] else near_recv).at[k],
                device_id=col_peer(*d), device_id_type=MESH).start()

    def wait_bytes(ref, sem):
        pltpu.make_async_copy(ref, ref, sem).wait()

    ids_copy = pltpu.make_async_remote_copy(
        src_ref=ids_src, dst_ref=ids_dst, send_sem=ids_send, recv_sem=ids_recv, device_id=partner, device_id_type=MESH)
    col_start(0)
    ids_copy.start()

    lane1 = lax.broadcasted_iota(jnp.int32, (1, BLK), 1)
    low_half = lane1 < NB

    v[...] = jnp.zeros((COLB, BLK), F32)
    start[0:1, :] = jnp.ones((1, BLK), F32)
    start[1:2, :] = jnp.zeros((1, BLK), F32)
    w[...] = jnp.zeros((16, BLK), F32)
    sol[...] = jnp.zeros((16, BLK), F32)
    col_dst[0, c] = col_src[0]
    loads[3].wait()
    loads[4].wait()
    loads[5].wait()

    def arrange(g, _):
        for t in range(2):
            i = g * 2 + t
            top = raw[pl.ds(i, NB, stride=BLK), :]
            low = raw[pl.ds(NB + i, NB, stride=BLK), :]
            tiles[i] = jnp.concatenate([top, low], axis=0).T
        return 0
    lax.fori_loop(0, NB // 2, arrange, 0)

    ids_copy.wait_recv()
    mine = ids_src[...]
    theirs = ids_dst[...]
    first = jnp.where(h == 0, mine, theirs)
    second = jnp.where(h == 0, theirs, mine)
    pair_cols = jnp.where(low_half, first, pltpu.roll(second, NB, 1))
    i256 = lax.broadcasted_iota(jnp.int32, (256, BLK), 0)
    owner_block = ((i256 // 16) * 32 + h * 16 + lax.rem(i256, 16)).astype(F32)
    put_cols[...] = jnp.where(owner_block == pair_cols, 1.0, 0.0).astype(BF16)

    wait_bytes(col_dst.at[0, pl.ds(0, 3)], near_recv.at[0])
    wait_bytes(col_dst.at[0, pl.ds(0, 4)], far_recv.at[0])
    for j in range(N_COL):
        u[j * PER_COL:(j + 1) * PER_COL, :] = col_dst[0, j, 0:PER_COL, :]
    row_number = lax.broadcasted_iota(jnp.int32, (ROWB, BLK), 0).astype(F32)

    def make_put_rows():
        for j in range(N_COL // 2):
            a = col_dst[0, 2 * j, NB:MSG, :]
            b = col_dst[0, 2 * j + 1, NB:MSG, :]
            pair = jnp.where(low_half, a, pltpu.roll(b, NB, 1))
            put_rows[j // 2, :, (j % 2) * BLK:(j % 2 + 1) * BLK] = jnp.where(row_number == pair, 1.0, 0.0).astype(BF16)

    def lsqr(k, rhobar, phibar, alpha, beta):
        unit = v[pl.ds(pl.multiple_of(r * 16, 16), 16), :] / alpha
        rho = jnp.sqrt(rhobar * rhobar + beta * beta)
        cosine = rhobar / rho
        sine = beta / rho
        theta = sine * alpha
        phi = cosine * phibar
        w_now = w[...]
        sol[...] = sol[...] + phi / rho * w_now
        w[...] = unit - theta / rho * w_now
        return jnp.where(k == 1, alpha, -cosine * alpha), jnp.where(k == 1, beta, sine * phibar)

    def step(k, carry):
        rhobar, phibar, beta_first, alpha_old, beta_old = carry
        su = total_of(u[...] * u[...])
        for n in range(NB):
            picks[n:n + 1, :] = u[pl.ds(rows_at[0, n], 1), :]
        chosen = picks[...]
        spread[...] = jnp.concatenate([chosen, pltpu.roll(chosen, NB, 1)], axis=0).T[0:NB, :]

        def back(g, acc):
            for t in range(UNROLL):
                i = g * UNROLL + t
                acc = acc + tiles[i] * spread[pl.ds(i, 1), :]
            return acc
        acc = lax.fori_loop(0, NB // UNROLL, back, jnp.zeros((BLK, BLK), F32)).T
        core_src[k, 0:NB, :] = acc[0:NB, :] + acc[NB:BLK, :]
        core_src[k, NB:MSG, :] = su
        swap = pltpu.make_async_remote_copy(
            src_ref=core_src.at[k], dst_ref=core_dst.at[k], send_sem=core_send.at[k], recv_sem=core_recv.at[k],
            device_id=partner, device_id_type=MESH)
        swap.start()
        for p, x in enumerate(split3(core_src[k, 0:NB, :])):
            parts2[pl.ds(pl.multiple_of(h * NB, NB), NB), p * BLK:(p + 1) * BLK] = x
        swap.wait_recv()
        for p, x in enumerate(split3(core_dst[k, 0:NB, :])):
            parts2[pl.ds(pl.multiple_of((1 - h) * NB, NB), NB), p * BLK:(p + 1) * BLK] = x
        dense = join3(jnp.dot(put_cols[...], parts2[...], preferred_element_type=F32))
        both = su + core_dst[k, NB:MSG, :]
        for j in range(N_CHIP):
            rs_src[k, j, 0:16, :] = dense[j * 16:(j + 1) * 16, :]
            rs_src[k, j, 16:PIECE, :] = both
        for d in CHIPS:
            pltpu.make_async_remote_copy(
                src_ref=rs_src.at[k, chip_at(*d)], dst_ref=rs_dst.at[k, q], send_sem=rs_send.at[k], recv_sem=rs_recv.at[k],
                device_id=row_peer(*d, 0), device_id_type=MESH).start()
        rs_dst[k, q] = rs_src[k, q]
        rhobar, phibar = lsqr(k, rhobar, phibar, alpha_old, beta_old)
        v[...] = v[...] * (1.0 / alpha_old)

        @pl.when(k == 0)
        def _():
            make_put_rows()
        wait_bytes(rs_dst.at[k, pl.ds(0, N_CHIP - 1)], rs_recv.at[k])
        piece = rs_dst[k, 0]
        for j in range(1, N_CHIP):
            piece = piece + rs_dst[k, j]
        vb[k, q, h] = piece[0:16, :]
        for d in CHIPS:
            pltpu.make_async_remote_copy(
                src_ref=vb.at[k, q, h], dst_ref=vb.at[k, q, h], send_sem=ag_send.at[k], recv_sem=ag_recv.at[k],
                device_id=row_peer(*d, 0), device_id_type=MESH).start()
        beta = jnp.sqrt(piece[16:17, :])
        inv_beta = 1.0 / beta
        u[...] = u[...] * inv_beta
        beta_first = jnp.where(k == 0, beta, beta_first)
        wait_bytes(vb.at[k, pl.ds(0, N_CHIP - 1), h], ag_recv.at[k])
        give = pltpu.make_async_remote_copy(
            src_ref=vb.at[k, :, h], dst_ref=vb.at[k, :, h], send_sem=half_send.at[k], recv_sem=half_recv.at[k],
            device_id=partner, device_id_type=MESH)
        give.start()

        def half_v(s):
            squares = jnp.zeros((16, BLK), F32)
            for j in range(N_CHIP):
                at = pl.ds(pl.multiple_of(j * 32 + s * 16, 16), 16)
                x = vb[k, j, s] * inv_beta - beta * v[at, :]
                v[at, :] = x
                squares = squares + x * x
            return total_of(squares)
        sv = half_v(h)
        give.wait_recv()
        sv = sv + half_v(1 - h)

        for n in range(NB):
            picks[n:n + 1, :] = v[pl.ds(cols_at[0, n], 1), :]
        chosen = picks[...]
        x = jnp.concatenate([chosen, chosen], axis=0).T

        def front(g, _):
            for t in range(UNROLL):
                i = g * UNROLL + t
                sums[pl.ds(pl.multiple_of(i * 8, 8), 8), :] = jnp.sum((tiles[i] * x).reshape(16, 8, BLK), axis=0)
            return 0
        lax.fori_loop(0, NB // UNROLL, front, 0)
        rows = sums[pl.ds(0, NB, stride=8), :]
        for s in range(1, 8):
            rows = rows + sums[pl.ds(s, NB, stride=8), :]
        rows = jnp.concatenate([rows, rows], axis=0).T
        col_src[k + 1, 0:NB, :] = jnp.where(low_half, rows[0:NB, :], rows[NB:BLK, :])
        col_src[k + 1, NB:MSG, :] = sv
        col_start(k + 1)
        col_dst[k + 1, c] = col_src[k + 1]

        def scatter(g):
            for j in range(4):
                for p, x in enumerate(split3(col_dst[k + 1, g * 4 + j, 0:NB, :])):
                    parts[g, j * NB:(j + 1) * NB, p * BLK:(p + 1) * BLK] = x
            return join3(jnp.dot(put_rows[g], parts[g], preferred_element_type=F32))
        wait_bytes(col_dst.at[k + 1, pl.ds(0, 3)], near_recv.at[k + 1])
        near = scatter(side)
        wait_bytes(col_dst.at[k + 1, pl.ds(0, 4)], far_recv.at[k + 1])
        far = scatter(1 - side)
        square = col_dst[k + 1, 0, NB:MSG, :]
        for j in range(1, N_COL):
            square = square + col_dst[k + 1, j, NB:MSG, :]
        alpha = jnp.sqrt(square)
        u[...] = (near + far) * (1.0 / alpha) - alpha * u[...]
        return rhobar, phibar, beta_first, alpha, beta

    one = start[0:1, :]
    rhobar, phibar, beta_first, alpha, beta = lax.fori_loop(0, ITERS, step, (one, start[1:2, :], one, one, one))

    su = total_of(u[...] * u[...])
    fin_src[...] = su
    for d in CORES:
        pltpu.make_async_remote_copy(
            src_ref=fin_src, dst_ref=fin_dst.at[r], send_sem=fin_send, recv_sem=fin_recv,
            device_id=row_peer(*d), device_id_type=MESH).start()
    fin_dst[r] = su
    rhobar, phibar = lsqr(ITERS, rhobar, phibar, alpha, beta)
    last = fin_dst.at[pl.ds(0, N_ROW - 1)]

    def drain(k, _):
        wait_bytes(core_dst.at[k], core_send.at[k])
        wait_bytes(rs_dst.at[k, pl.ds(0, N_CHIP - 1)], rs_send.at[k])
        wait_bytes(vb.at[k, pl.ds(0, N_CHIP - 1), h], ag_send.at[k])
        wait_bytes(vb.at[k, :, h], half_send.at[k])
        wait_bytes(col_dst.at[k, pl.ds(0, N_COL - 1)], col_send.at[k])
        return 0
    lax.fori_loop(0, ITERS, drain, 0)
    wait_bytes(col_dst.at[ITERS, pl.ds(0, N_COL - 1)], col_send.at[ITERS])
    ids_copy.wait_send()

    wait_bytes(last, fin_recv)
    square = fin_dst[0]
    for j in range(1, N_ROW):
        square = square + fin_dst[j]
    beta = jnp.sqrt(square)
    rho = jnp.sqrt(rhobar * rhobar + beta * beta)
    phi = rhobar / rho * phibar
    sol_out[...] = sol[...] + phi / rho * w[...]
    rel_out[...] = jnp.broadcast_to(beta / rho * phibar / beta_first, (8, BLK))
    wait_bytes(last, fin_send)


def on_device(rhs, blocks, blk_row, blk_col):
    vmem = pl.BlockSpec(memory_space=pltpu.VMEM)
    hbm = pl.BlockSpec(memory_space=pl.ANY)
    dma = pltpu.SemaphoreType.DMA
    many = dma((ITERS + 1,))
    sol, rel = pl.pallas_call(
        kernel,
        out_shape=(jax.ShapeDtypeStruct((16, BLK), F32), jax.ShapeDtypeStruct((8, BLK), F32)),
        in_specs=[hbm, hbm, hbm, hbm],
        out_specs=(vmem, vmem),
        scratch_shapes=[
            pltpu.VMEM((NB * BLK, BLK), F32),
            pltpu.VMEM((NB, BLK, BLK), F32),
            pltpu.VMEM((ROWB, BLK), F32),
            pltpu.VMEM((COLB, BLK), F32),
            pltpu.VMEM((NB, BLK), F32),
            pltpu.VMEM((NB, BLK), F32),
            pltpu.VMEM((NB * 8, BLK), F32),
            pltpu.VMEM((2, ROWB, 256), BF16),
            pltpu.VMEM((256, BLK), BF16),
            pltpu.VMEM((2, 256, 3 * BLK), BF16),
            pltpu.VMEM((2 * NB, 3 * BLK), BF16),
            pltpu.VMEM((ITERS + 1, MSG, BLK), F32),
            pltpu.VMEM((ITERS + 1, N_COL, MSG, BLK), F32),
            pltpu.VMEM((ITERS, MSG, BLK), F32),
            pltpu.VMEM((ITERS, MSG, BLK), F32),
            pltpu.VMEM((ITERS, N_CHIP, PIECE, BLK), F32),
            pltpu.VMEM((ITERS, N_CHIP, PIECE, BLK), F32),
            pltpu.VMEM((ITERS, N_CHIP, 2, 16, BLK), F32),
            pltpu.VMEM((1, BLK), F32),
            pltpu.VMEM((1, BLK), F32),
            pltpu.VMEM((1, BLK), F32),
            pltpu.VMEM((N_ROW, 1, BLK), F32),
            pltpu.VMEM((16, BLK), F32),
            pltpu.VMEM((16, BLK), F32),
            pltpu.VMEM((8, BLK), F32),
            pltpu.VMEM((1, NB), jnp.int32),
            pltpu.VMEM((1, NB), jnp.int32),
            pltpu.SMEM((1, NB), jnp.int32),
            pltpu.SMEM((1, NB), jnp.int32),
            dma((6,)), many, many, many, many, many, many, many, many, many, many, many, dma, dma, dma, dma,
        ],
        compiler_params=pltpu.CompilerParams(
            collective_id=0, has_side_effects=True, vmem_limit_bytes=60 * 1024 * 1024),
    )(blk_row.reshape(1, NB), blk_col.reshape(1, NB), rhs.reshape(PER_COL, BLK), blocks.reshape(NB * BLK, BLK))
    return sol.reshape(16 * BLK), rel[0, 0]


def solution(mesh):
    return jax.shard_map(
        on_device,
        mesh=mesh,
        in_specs=(
            P(("row", "col")),
            P("row", "col", None, None, None),
            P("row", "col", None),
            P("row", "col", None),
        ),
        out_specs=(P(("col", "row")), P()),
        check_vma=False,
    )
```

time: 1730 us -> 88.5 us (0.05)
  waiting for transfers between devices: 898 us -> 0 us
  blocking collectives: 733 us -> 0 us
  Pallas kernels: 0 us -> 85.2 us
  matrix products: 40.7 us -> 0 us
  other arithmetic: 25.8 us -> 0 us
  between operations: 22.1 us -> 0.64 us
    unnamed x12 -> x0, waiting for transfers between devices: 898 us -> none
    psum x7 -> x0, blocking collectives: 553 us -> none  [u_length(): return jnp.sqrt(lax.psum(jnp.sum(vec * vec), ('row', 'col')))]
    all_gather x6 -> x0, blocking collectives: 180 us -> none  [the longest x3 95.7 us: forward(): whole = lax.all_gather(vec, 'row', axis=0, tiled=True)]
    pallas_call x0 -> x1, Pallas kernels: none -> 85.2 us  [on_device(): pl.pallas_call(kernel, out_shape=(jax.ShapeDtypeStruct((16, BLK), F32), j...]
    dot_general x6 -> x0, matrix products: 40.7 us -> none  [the longest x3 24.9 us: fwd_local(): jnp.einsum('nij,nj->ni', tiles, picked, precision=lax.Precision.HIGHEST)]
  transfers between devices with their start and end apart: 6 -> 0, of which waited for: 6 -> 0; matrix products, arithmetic and copies ran while one was open for 0% -> 0% of each run, Pallas kernels for 0% -> 0%
where the time goes in v2:
time: 88.5 us; the launch traced here: 88.3 us
  Pallas kernels  85.2 us (96%)
  local copies, waits for them, and re-layouts  2.48 us (3%)
    pallas_call x1, Pallas kernels, on_device(): pl.pallas_call(kernel, out_shape=(jax.ShapeDtypeStruct((16, BLK), F32), j...  85.2 us

profile of v2, /device:TPU:1, one launch (start us, length us, event | category | flops | bytes accessed | tf_op | source)
XLA Modules:
  0.0 88.3 jit_solution(11652662237441563149)
XLA Ops:
  0.6 85.2 %shard_map.59 = (f32[16,128]{1,0:T(8,128)}, f32[8,128]{1,0:T(8,128)}) custom-call(s32[1,64]{1,0:T(1,128)} %bitcast.9, s32[1,64]{1,0:T(1,128)} %bitcast.10, f32[62,128]{1,0:T(8,128)} %bitcast.7, f32[8192,128]{1,0:T(8,128)} %bitcast.6), custom_call_target="tpu_custom_call" | custom-call | tf_op jit(solution)/shard_map/pallas_call | solution.py:323
  85.8 1.2 %slice.3 = f32[1,1]{1,0:T(1,128)} slice(f32[8,128]{1,0:T(8,128)} %get-tuple-element.5), slice={[0:1], [0:1]} | slice | bytes 8 | tf_op jit(solution)/shard_map/slice | solution.py:363
  87.0 1.3 %copy.7 = f32[2048]{0:T(1024)} copy(f32[2048]{0:T(1024)} %bitcast.8) | data formatting | bytes 16384

commit v3 on v2

--- a/solution.py
+++ b/solution.py
@@ -322,7 +322,7 @@
     many = dma((ITERS + 1,))
     sol, rel = pl.pallas_call(
         kernel,
-        out_shape=(jax.ShapeDtypeStruct((16, BLK), F32), jax.ShapeDtypeStruct((8, BLK), F32)),
+        out_shape=(pltpu.VMEM((16, BLK), F32), pltpu.VMEM((8, BLK), F32)),
         in_specs=[hbm, hbm, hbm, hbm],
         out_specs=(vmem, vmem),
         scratch_shapes=[

time: 88.5 us -> 86.1 us (0.973)
  local copies, waits for them, and re-layouts: 2.48 us -> 1.11 us
  Pallas kernels: 85.2 us -> 83.9 us
    pallas_call x1, Pallas kernels: 85.2 us -> 83.9 us  [on_device(): pl.pallas_call(kernel, out_shape=(pltpu.VMEM((16, BLK), F32), pltpu.VMEM(...]
where the time goes in v3:
time: 86.1 us; the launch traced here: 85.7 us
  Pallas kernels  83.9 us (97%)
  local copies, waits for them, and re-layouts  1.11 us (1%)
    pallas_call x1, Pallas kernels, on_device(): pl.pallas_call(kernel, out_shape=(pltpu.VMEM((16, BLK), F32), pltpu.VMEM(...  83.9 us

profile of v3, /device:TPU:1, one launch (start us, length us, event | category | flops | bytes accessed | tf_op | source)
XLA Modules:
  0.0 85.7 jit_solution(1310642663110786635)
XLA Ops:
  0.6 83.9 %shard_map.59 = (f32[16,128]{1,0:T(8,128)S(1)}, f32[8,128]{1,0:T(8,128)S(1)}) custom-call(s32[1,64]{1,0:T(1,128)} %bitcast.9, s32[1,64]{1,0:T(1,128)} %bitcast.10, f32[62,128]{1,0:T(8,128)} %bitcast.8, f32[8192,128]{1,0:T(8,128)} %bitcast.7), custom_call_target="tpu_custom_call" | custom-call | tf_op jit(solution)/shard_map/pallas_call | solution.py:323
  84.6 0.5 slice.3
  85.1 0.6 copy.7

commit v4 on v3

--- a/solution.py
+++ b/solution.py
@@ -19,7 +19,7 @@
 BF16 = jnp.bfloat16
 MSG = NB + 1
 PIECE = 17
-UNROLL = 8
+UNROLL = 32
 
 
 def ring(d, n):
@@ -50,11 +50,11 @@
 
 
 def kernel(rows_hbm, cols_hbm, rhs_hbm, blocks_hbm, sol_out, rel_out,
-           raw, tiles, u, v, picks, spread, sums, put_rows, put_cols, parts, parts2,
-           col_src, col_dst, core_src, core_dst, rs_src, rs_dst, vb, ids_src, ids_dst, fin_src, fin_dst, w, sol, start,
+           raw, tiles, u, v, picks, u_picks, near_sum, spread, sums, put_rows, pick_rows, put_cols, parts, parts2,
+           col_src, col_dst, core_src, core_dst, rs_src, rs_dst, half_src, half_dst, vb, ids_src, ids_dst, fin_src, fin_dst, w, sol, start,
            rows_v, cols_v, rows_at, cols_at,
            load_sem, col_send, near_recv, far_recv, core_send, core_recv, rs_send, rs_recv, ag_send, ag_recv,
-           half_send, half_recv, ids_send, ids_recv, fin_send, fin_recv):
+           norm_send, norm_recv, half_send, half_recv, ids_send, ids_recv, fin_send, fin_recv):
     r = lax.axis_index("row")
     c = lax.axis_index("col")
     q = r // 2
@@ -153,11 +153,14 @@
     row_number = lax.broadcasted_iota(jnp.int32, (ROWB, BLK), 0).astype(F32)
 
     def make_put_rows():
+        own_rows = jnp.broadcast_to(col_src[0, NB:MSG, :], (BLK, BLK)).T[0:NB, :]
         for j in range(N_COL // 2):
             a = col_dst[0, 2 * j, NB:MSG, :]
             b = col_dst[0, 2 * j + 1, NB:MSG, :]
             pair = jnp.where(low_half, a, pltpu.roll(b, NB, 1))
-            put_rows[j // 2, :, (j % 2) * BLK:(j % 2 + 1) * BLK] = jnp.where(row_number == pair, 1.0, 0.0).astype(BF16)
+            lanes = slice((j % 2) * BLK, (j % 2 + 1) * BLK)
+            put_rows[j // 2, :, lanes] = jnp.where(row_number == pair, 1.0, 0.0).astype(BF16)
+            pick_rows[j // 2, :, lanes] = jnp.where(own_rows == pair, 1.0, 0.0).astype(BF16)
 
     def lsqr(k, rhobar, phibar, alpha, beta):
         unit = v[pl.ds(pl.multiple_of(r * 16, 16), 16), :] / alpha
@@ -171,12 +174,16 @@
         w[...] = unit - theta / rho * w_now
         return jnp.where(k == 1, alpha, -cosine * alpha), jnp.where(k == 1, beta, sine * phibar)
 
+    for n in range(NB):
+        u_picks[n:n + 1, :] = u[pl.ds(rows_at[0, n], 1), :]
+
+    def finish_u(alpha):
+        far = join3(jnp.dot(put_rows[1 - side], parts[1 - side], preferred_element_type=F32))
+        u[...] = (near_sum[...] + far) * (1.0 / alpha) - alpha * u[...]
+
     def step(k, carry):
         rhobar, phibar, beta_first, alpha_old, beta_old = carry
-        su = total_of(u[...] * u[...])
-        for n in range(NB):
-            picks[n:n + 1, :] = u[pl.ds(rows_at[0, n], 1), :]
-        chosen = picks[...]
+        chosen = u_picks[...]
         spread[...] = jnp.concatenate([chosen, pltpu.roll(chosen, NB, 1)], axis=0).T[0:NB, :]
 
         def back(g, acc):
@@ -185,22 +192,25 @@
                 acc = acc + tiles[i] * spread[pl.ds(i, 1), :]
             return acc
         acc = lax.fori_loop(0, NB // UNROLL, back, jnp.zeros((BLK, BLK), F32)).T
-        core_src[k, 0:NB, :] = acc[0:NB, :] + acc[NB:BLK, :]
-        core_src[k, NB:MSG, :] = su
+        core_src[k] = acc[0:NB, :] + acc[NB:BLK, :]
         swap = pltpu.make_async_remote_copy(
             src_ref=core_src.at[k], dst_ref=core_dst.at[k], send_sem=core_send.at[k], recv_sem=core_recv.at[k],
             device_id=partner, device_id_type=MESH)
         swap.start()
-        for p, x in enumerate(split3(core_src[k, 0:NB, :])):
+        for p, x in enumerate(split3(core_src[k])):
             parts2[pl.ds(pl.multiple_of(h * NB, NB), NB), p * BLK:(p + 1) * BLK] = x
+
+        @pl.when(k > 0)
+        def _():
+            finish_u(alpha_old)
+        su = total_of(u[...] * u[...])
         swap.wait_recv()
-        for p, x in enumerate(split3(core_dst[k, 0:NB, :])):
+        for p, x in enumerate(split3(core_dst[k])):
             parts2[pl.ds(pl.multiple_of((1 - h) * NB, NB), NB), p * BLK:(p + 1) * BLK] = x
         dense = join3(jnp.dot(put_cols[...], parts2[...], preferred_element_type=F32))
-        both = su + core_dst[k, NB:MSG, :]
         for j in range(N_CHIP):
             rs_src[k, j, 0:16, :] = dense[j * 16:(j + 1) * 16, :]
-            rs_src[k, j, 16:PIECE, :] = both
+            rs_src[k, j, 16:PIECE, :] = su
         for d in CHIPS:
             pltpu.make_async_remote_copy(
                 src_ref=rs_src.at[k, chip_at(*d)], dst_ref=rs_dst.at[k, q], send_sem=rs_send.at[k], recv_sem=rs_recv.at[k],
@@ -221,9 +231,16 @@
             pltpu.make_async_remote_copy(
                 src_ref=vb.at[k, q, h], dst_ref=vb.at[k, q, h], send_sem=ag_send.at[k], recv_sem=ag_recv.at[k],
                 device_id=row_peer(*d, 0), device_id_type=MESH).start()
-        beta = jnp.sqrt(piece[16:17, :])
+        half_src[k] = piece[16:17, :]
+        norm = pltpu.make_async_remote_copy(
+            src_ref=half_src.at[k], dst_ref=half_dst.at[k], send_sem=norm_send.at[k], recv_sem=norm_recv.at[k],
+            device_id=partner, device_id_type=MESH)
+        norm.start()
+        norm.wait_recv()
+        beta = jnp.sqrt(half_src[k] + half_dst[k])
         inv_beta = 1.0 / beta
         u[...] = u[...] * inv_beta
+        u_picks[...] = u_picks[...] * inv_beta
         beta_first = jnp.where(k == 0, beta, beta_first)
         wait_bytes(vb.at[k, pl.ds(0, N_CHIP - 1), h], ag_recv.at[k])
         give = pltpu.make_async_remote_copy(
@@ -267,21 +284,23 @@
             for j in range(4):
                 for p, x in enumerate(split3(col_dst[k + 1, g * 4 + j, 0:NB, :])):
                     parts[g, j * NB:(j + 1) * NB, p * BLK:(p + 1) * BLK] = x
-            return join3(jnp.dot(put_rows[g], parts[g], preferred_element_type=F32))
+            return join3(jnp.dot(pick_rows[g], parts[g], preferred_element_type=F32))
         wait_bytes(col_dst.at[k + 1, pl.ds(0, 3)], near_recv.at[k + 1])
         near = scatter(side)
+        near_sum[...] = join3(jnp.dot(put_rows[side], parts[side], preferred_element_type=F32))
         wait_bytes(col_dst.at[k + 1, pl.ds(0, 4)], far_recv.at[k + 1])
         far = scatter(1 - side)
         square = col_dst[k + 1, 0, NB:MSG, :]
         for j in range(1, N_COL):
             square = square + col_dst[k + 1, j, NB:MSG, :]
         alpha = jnp.sqrt(square)
-        u[...] = (near + far) * (1.0 / alpha) - alpha * u[...]
+        u_picks[...] = (near + far) * (1.0 / alpha) - alpha * u_picks[...]
         return rhobar, phibar, beta_first, alpha, beta
 
     one = start[0:1, :]
     rhobar, phibar, beta_first, alpha, beta = lax.fori_loop(0, ITERS, step, (one, start[1:2, :], one, one, one))
 
+    finish_u(alpha)
     su = total_of(u[...] * u[...])
     fin_src[...] = su
     for d in CORES:
@@ -294,6 +313,7 @@
 
     def drain(k, _):
         wait_bytes(core_dst.at[k], core_send.at[k])
+        wait_bytes(half_dst.at[k], norm_send.at[k])
         wait_bytes(rs_dst.at[k, pl.ds(0, N_CHIP - 1)], rs_send.at[k])
         wait_bytes(vb.at[k, pl.ds(0, N_CHIP - 1), h], ag_send.at[k])
         wait_bytes(vb.at[k, :, h], half_send.at[k])
@@ -332,17 +352,22 @@
             pltpu.VMEM((COLB, BLK), F32),
             pltpu.VMEM((NB, BLK), F32),
             pltpu.VMEM((NB, BLK), F32),
+            pltpu.VMEM((ROWB, BLK), F32),
+            pltpu.VMEM((NB, BLK), F32),
             pltpu.VMEM((NB * 8, BLK), F32),
             pltpu.VMEM((2, ROWB, 256), BF16),
+            pltpu.VMEM((2, NB, 256), BF16),
             pltpu.VMEM((256, BLK), BF16),
             pltpu.VMEM((2, 256, 3 * BLK), BF16),
             pltpu.VMEM((2 * NB, 3 * BLK), BF16),
             pltpu.VMEM((ITERS + 1, MSG, BLK), F32),
             pltpu.VMEM((ITERS + 1, N_COL, MSG, BLK), F32),
-            pltpu.VMEM((ITERS, MSG, BLK), F32),
-            pltpu.VMEM((ITERS, MSG, BLK), F32),
+            pltpu.VMEM((ITERS, NB, BLK), F32),
+            pltpu.VMEM((ITERS, NB, BLK), F32),
             pltpu.VMEM((ITERS, N_CHIP, PIECE, BLK), F32),
             pltpu.VMEM((ITERS, N_CHIP, PIECE, BLK), F32),
+            pltpu.VMEM((ITERS, 1, BLK), F32),
+            pltpu.VMEM((ITERS, 1, BLK), F32),
             pltpu.VMEM((ITERS, N_CHIP, 2, 16, BLK), F32),
             pltpu.VMEM((1, BLK), F32),
             pltpu.VMEM((1, BLK), F32),
@@ -355,7 +380,7 @@
             pltpu.VMEM((1, NB), jnp.int32),
             pltpu.SMEM((1, NB), jnp.int32),
             pltpu.SMEM((1, NB), jnp.int32),
-            dma((6,)), many, many, many, many, many, many, many, many, many, many, many, dma, dma, dma, dma,
+            dma((6,)), many, many, many, many, many, many, many, many, many, many, many, many, many, dma, dma, dma, dma,
         ],
         compiler_params=pltpu.CompilerParams(
             collective_id=0, has_side_effects=True, vmem_limit_bytes=60 * 1024 * 1024),

time: 86.1 us -> 86 us (level)
  no operation moved by 1% of the time
where the time goes in v4:
time: 86 us; the launch traced here: 85.9 us
  Pallas kernels  84.1 us (98%)
  local copies, waits for them, and re-layouts  1.11 us (1%)
    pallas_call x1, Pallas kernels, on_device(): pl.pallas_call(kernel, out_shape=(pltpu.VMEM((16, BLK), F32), pltpu.VMEM(...  84.1 us

profile of v4, /device:TPU:1, one launch (start us, length us, event | category | flops | bytes accessed | tf_op | source)
XLA Modules:
  0.0 85.9 jit_solution(14197401661856403723)
XLA Ops:
  0.6 84.1 %shard_map.59 = (f32[16,128]{1,0:T(8,128)S(1)}, f32[8,128]{1,0:T(8,128)S(1)}) custom-call(s32[1,64]{1,0:T(1,128)} %bitcast.9, s32[1,64]{1,0:T(1,128)} %bitcast.10, f32[62,128]{1,0:T(8,128)} %bitcast.8, f32[8192,128]{1,0:T(8,128)} %bitcast.7), custom_call_target="tpu_custom_call" | custom-call | tf_op jit(solution)/shard_map/pallas_call | solution.py:343
  84.8 0.5 slice.3
  85.3 0.6 copy.7

commit v5 on v3

--- a/solution.py
+++ b/solution.py
@@ -74,12 +74,6 @@
     def col_peer(dx, dy):
         return {"row": r, "col": lax.rem(side + dx, 2) * 4 + lax.rem(y + dy, 4)}
 
-    barrier = pltpu.get_barrier_semaphore()
-    for d in CORES:
-        pl.semaphore_signal(barrier, inc=1, device_id=row_peer(*d), device_id_type=MESH)
-    for d in COLS:
-        pl.semaphore_signal(barrier, inc=1, device_id=col_peer(*d), device_id_type=MESH)
-
     loads = [
         pltpu.make_async_copy(rows_hbm, rows_v, load_sem.at[0]),
         pltpu.make_async_copy(cols_hbm, cols_v, load_sem.at[1]),
@@ -90,6 +84,11 @@
     ]
     for copy in loads:
         copy.start()
+    barrier = pltpu.get_barrier_semaphore()
+    for d in CORES:
+        pl.semaphore_signal(barrier, inc=1, device_id=row_peer(*d), device_id_type=MESH)
+    for d in COLS:
+        pl.semaphore_signal(barrier, inc=1, device_id=col_peer(*d), device_id_type=MESH)
     col_src[0, PER_COL:MSG, :] = jnp.zeros((MSG - PER_COL, BLK), F32)
     ids_src[...] = jnp.zeros((1, BLK), F32)
     loads[0].wait()

time: 86.1 us -> 86.4 us (level)
  no operation moved by 1% of the time
where the time goes in v5:
time: 86.4 us
  Pallas kernels  84.6 us (98%)
  local copies, waits for them, and re-layouts  1.11 us (1%)
    pallas_call x1, Pallas kernels, on_device(): pl.pallas_call(kernel, out_shape=(pltpu.VMEM((16, BLK), F32), pltpu.VMEM(...  84.6 us

profile of v5, /device:TPU:1, one launch (start us, length us, event | category | flops | bytes accessed | tf_op | source)
XLA Modules:
  0.0 86.4 jit_solution(12137101346011084706)
XLA Ops:
  0.6 84.6 %shard_map.59 = (f32[16,128]{1,0:T(8,128)S(1)}, f32[8,128]{1,0:T(8,128)S(1)}) custom-call(s32[1,64]{1,0:T(1,128)} %bitcast.9, s32[1,64]{1,0:T(1,128)} %bitcast.10, f32[62,128]{1,0:T(8,128)} %bitcast.8, f32[8192,128]{1,0:T(8,128)} %bitcast.7), custom_call_target="tpu_custom_call" | custom-call | tf_op jit(solution)/shard_map/pallas_call | solution.py:322
  85.3 0.5 slice.3
  85.8 0.6 copy.7
